TPU v7x, 256 devices: a whole 4x4x8 slice. The times are simulated.
256 devices in a mesh: dp: 32 (over x, y, core), ctx: 8 (over z).
Axes of the slice: x: 4, y: 4, z: 8, core: 2. Of those that a mesh axis runs over, the one named last changes fastest.
Arguments:
- cotangent: bfloat16 [32, 4096, 8192], P('dp', 'ctx'), may hold values from -6 to 6
- out_weight: bfloat16 [256, 8192], P(None, 'ctx'), may hold values from -0.0625 to 0.0625
- head_input: bfloat16 [32, 4096, 256], P('dp', 'ctx'), may hold values from -6 to 6
- injector: bfloat16 [32, 4096, 128], P('dp', 'ctx'), may hold values from -0.59765625 to 0.59765625
- readout: bfloat16 [32, 4096, 128], P('dp', 'ctx'), may hold values from -0.59765625 to 0.59765625
- decay_code: int32 [32, 4096, 2], P('dp', 'ctx'), may hold values from 1 to 40960
- decay_rate: float32 [2], replicated, may hold values from 4.8828125e-06 to 0.0061035156
- start_state: float32 [32, 8, 2, 128, 128], P('dp', 'ctx'), may hold values from -6 to 6
Outputs:
- gradient_input: bfloat16 [32, 4096, 256], P('dp', 'ctx')
- gradient_injector: float32 [32, 4096, 128], P('dp', 'ctx')
- gradient_readout: float32 [32, 4096, 128], P('dp', 'ctx')
- gradient_weight: float32 [256, 8192], P('ctx', 'dp')
- gradient_rate: float32 [2], replicated
All inputs are finite; a program needn't handle non-finite values.
Results may differ from a plain program's by a relative error of at most 0.0049.
Values may be sent and summed in bfloat16 or wider, within the bound.
No kernel may reach another device: no remote copies, remote signals or barrier semaphores. Data moves between devices by JAX's collectives and lax.ppermute only.
A program may use at most 128 MiB of HBM per device.

v0:
```python
import jax
import jax.numpy as jnp
from jax import lax
from jax.sharding import PartitionSpec as P

precise = lax.Precision.HIGHEST


def carried_in(value, axis, join, neutral):
    count, mine = (lax.axis_size(axis), lax.axis_index(axis))
    pieces = jax.tree.map(lambda part: lax.all_gather(part, axis), value)
    pieces = jax.tree.map(lambda part: part[::-1], pieces)
    mine = count - 1 - mine
    total = jax.tree.map(
        lambda part, zero: jnp.full_like(part, 0) + jnp.asarray(zero, part.dtype), value, neutral
    )

    def lap(position, total):
        longer = join(total, jax.tree.map(lambda part: part[position], pieces))
        return jax.tree.map(lambda new, old: jnp.where(position < mine, new, old), longer, total)

    return lax.fori_loop(0, count - 1, lap, total)


def decay_table(log_decay):
    cumulative = jnp.cumsum(log_decay, axis=0)
    length = log_decay.shape[0]
    row_index = lax.broadcasted_iota(jnp.int32, (length, length), 0)
    col_index = lax.broadcasted_iota(jnp.int32, (length, length), 1)
    causal = (row_index >= col_index)[None]
    spread = cumulative.T[:, :, None] - cumulative.T[:, None, :]
    weights = jnp.where(causal, jnp.exp(jnp.where(causal, spread, 0.0)), 0.0)
    return (cumulative, weights)


def forward_shard(head_input, injector, readout, log_decay, start_state):
    length, heads_count = log_decay.shape
    cumulative, weights = decay_table(log_decay)
    intersection = jnp.dot(readout, injector.T, preferred_element_type=jnp.float32)
    mixing = intersection[None] * weights
    inputs_heads = head_input.reshape(length, heads_count, -1).astype(jnp.float32)
    within = jnp.einsum("hts,shp->thp", mixing, inputs_heads, precision=precise)
    carried = jnp.einsum("tn,hpn->thp", readout.astype(jnp.float32), start_state, precision=precise)
    outputs = within + jnp.exp(cumulative)[:, :, None] * carried
    return outputs.reshape(length, -1).astype(jnp.bfloat16)


def chain_piece(readout, output_grad, log_decay):
    length, heads_count = log_decay.shape
    cumulative = jnp.cumsum(log_decay, axis=0)
    grad_heads = output_grad.reshape(length, heads_count, -1).astype(jnp.float32)
    scaled = jnp.exp(cumulative)[:, :, None] * readout.astype(jnp.float32)[:, None, :]
    adjoint = jnp.einsum("thp,thn->hpn", grad_heads, scaled, precision=precise)
    return (jnp.exp(cumulative[-1]), adjoint)


def backward_shard(head_input, injector, readout, output_grad, log_decay, start_state, incoming):
    length, heads_count = log_decay.shape
    cumulative, weights = decay_table(log_decay)
    inputs_narrow = head_input.reshape(length, heads_count, -1)
    grad_narrow = output_grad.reshape(length, heads_count, -1)
    inputs_heads = inputs_narrow.astype(jnp.float32)
    grad_heads = grad_narrow.astype(jnp.float32)
    inject_float = injector.astype(jnp.float32)
    read_float = readout.astype(jnp.float32)
    intersection = jnp.dot(readout, injector.T, preferred_element_type=jnp.float32)
    mixing = intersection[None] * weights
    to_end = jnp.exp(cumulative[-1][None, :] - cumulative)
    from_start = jnp.exp(cumulative)
    entering = jnp.einsum("sn,hpn->shp", inject_float, incoming, precision=precise)
    grad_input = (
        jnp.einsum("hts,thp->shp", mixing, grad_heads, precision=precise)
        + to_end[:, :, None] * entering
    )
    pairing = (
        jnp.einsum("thp,shp->hts", grad_narrow, inputs_narrow, preferred_element_type=jnp.float32)
        * weights
    )
    through_start = jnp.einsum("thp,hpn->thn", grad_heads, start_state, precision=precise)
    grad_read = jnp.einsum("hts,sn->tn", pairing, inject_float, precision=precise)
    grad_read = grad_read + jnp.einsum("th,thn->tn", from_start, through_start, precision=precise)
    input_state = jnp.einsum("shp,hpn->shn", inputs_heads, incoming, precision=precise)
    grad_inject = jnp.einsum("hts,tn->sn", pairing, read_float, precision=precise)
    grad_inject = grad_inject + jnp.einsum("sh,shn->sn", to_end, input_state, precision=precise)
    products = intersection[None] * pairing
    carried = (
        jnp.einsum("tn,hpn->thp", read_float, start_state, precision=precise)
        * from_start[:, :, None]
    )
    reaching = to_end * jnp.einsum("shn,sn->sh", input_state, inject_float, precision=precise)
    end_term = from_start[-1] * jnp.einsum(
        "hpn,hpn->h", incoming, start_state, precision=precise
    ) + jnp.sum(reaching, axis=0)
    cumul_grad = jnp.sum(products, axis=2).T - jnp.sum(products, axis=1).T
    cumul_grad = cumul_grad + jnp.sum(grad_heads * carried, axis=2) - reaching
    is_last = lax.broadcasted_iota(jnp.int32, (length, 1), 0) == length - 1
    cumul_grad = cumul_grad + jnp.where(is_last, end_term[None, :], 0.0)
    decay_grad = jnp.flip(jnp.cumsum(jnp.flip(cumul_grad, 0), axis=0), 0)
    rate_terms = jnp.sum(decay_grad * log_decay, axis=0)
    return (grad_input.reshape(length, -1).astype(jnp.bfloat16), grad_inject, grad_read, rate_terms)


def combine(earlier, later):
    return (later[0] * earlier[0], later[1] + later[0][:, None, None] * earlier[1])


def local(
    cotangent, out_weight, head_input, injector, readout, decay_code, decay_rate, start_state
):
    grad_out = cotangent[0]
    inputs_local = head_input[0]
    inject_local = injector[0]
    read_local = readout[0]
    state_local = start_state[0, 0]
    length = grad_out.shape[0]
    output_grad = lax.dot_general(
        grad_out,
        lax.all_gather(out_weight, "ctx", axis=1, tiled=True),
        (((1,), (1,)), ((), ())),
        preferred_element_type=jnp.float32,
    ).astype(jnp.bfloat16)
    log_decay = -decay_rate[None, :] * decay_code[0].astype(jnp.float32)
    decay_total, adjoint = chain_piece(read_local, output_grad, log_decay)
    identity = (jnp.ones_like(decay_total), jnp.zeros_like(adjoint))
    incoming = carried_in((decay_total, adjoint), "ctx", combine, identity)[1]
    outputs = forward_shard(inputs_local, inject_local, read_local, log_decay, state_local)
    local_weight = lax.dot_general(
        outputs, grad_out, (((0,), (0,)), ((), ())), preferred_element_type=jnp.float32
    )
    data_part = lax.psum_scatter(local_weight, "dp", scatter_dimension=1, tiled=True)
    weight_part = lax.psum_scatter(data_part, "ctx", scatter_dimension=0, tiled=True)
    grad_input, grad_inject, grad_read, rate_terms = backward_shard(
        inputs_local, inject_local, read_local, output_grad, log_decay, state_local, incoming
    )
    tokens_all = length * lax.axis_size("dp") * lax.axis_size("ctx")
    rate_sum = lax.psum(rate_terms, ("dp", "ctx"))
    return (
        grad_input[None],
        grad_inject[None],
        grad_read[None],
        weight_part,
        rate_sum / tokens_all,
    )


def solution(mesh):
    in_specs = (
        P("dp", "ctx", None),
        P(None, "ctx"),
        P("dp", "ctx", None),
        P("dp", "ctx", None),
        P("dp", "ctx", None),
        P("dp", "ctx", None),
        P(),
        P("dp", "ctx", None, None, None),
    )
    out_specs = (
        P("dp", "ctx", None),
        P("dp", "ctx", None),
        P("dp", "ctx", None),
        P("ctx", "dp"),
        P(),
    )
    return jax.shard_map(local, mesh=mesh, in_specs=in_specs, out_specs=out_specs, check_vma=False)
```

profile of v0, /device:TPU:2, one launch (start us, length us, event | category | flops | bytes accessed | tf_op | source)
XLA Modules:
  0.0 262.4 jit_solution(3269358175071123547)
XLA Ops:
  7.2 0.7 all-gather.5.cloned.1.call-update
  7.9 0.7 neg.4
  8.6 0.8 fusion.61
  9.4 0.6 reduce-window.14
  10.3 0.9 bitcast_convert_fusion.1
  11.5 56.1 %all-gather.5.cloned.1.call-done = bf16[256,8192]{1,0:T(8,128)(2,1)} async-done(((bf16[256,1024]{1,0:T(8,128)(2,1)}), bf16[256,8192]{1,0:T(8,128)(2,1)}) %all-gather.5.cloned.1.call-update) | async-done | bytes 4194320 | tf_op jit(solution)/shard_map/all_gather | solution.py:118
  67.6 6.9 %fusion.26 = bf16[512,256]{0,1:T(8,128)(2,1)S(1)} fusion(bf16[256,8192]{1,0:T(8,128)(2,1)} %all-gather.5.cloned.1.call-done, bf16[1,512,8192]{2,1,0:T(8,128)(2,1)} %param.10), kind=kOutput, calls=%fused_computation.24 | convolution fusion | flops 2147614720 | bytes 12845056 | tf_op jit(solution)/shard_map/dot_general | solution.py:116
  74.6 1.1 fusion.43
  76.8 2.0 fusion.22
  78.7 9.1 %fusion.1 = f32[256,8192]{1,0:T(8,128)} fusion(bf16[512,256]{0,1:T(8,128)(2,1)S(1)} %bitcast.164, bf16[1,512,8192]{2,1,0:T(8,128)(2,1)} %param.10), kind=kOutput, calls=%fused_computation.3 | convolution fusion | flops 2147483648 | bytes 17039360 | tf_op jit(solution)/shard_map/dot_general | solution.py:127
  88.0 14.7 %all-gather.1 = f32[8,1,2]{2,1,0:T(1,128)S(1)} all-gather(f32[1,1,2]{2,1,0:T(1,128)S(1)} %bitcast.175), channel_id=1, replica_groups=mesh['dp'=32,'ctx'=8] {'ctx'}, dimensions={0}, use_global_device_ids=true | all-gather | bytes 72 | tf_op jit(solution)/shard_map/all_gather | solution.py:11
  104.0 4.4 %fusion.45 = f32[512,1,128]{2,1,0:T(1,128)} fusion(f32[512,2,1]{1,2,0:T(1,128)S(1)} %copy.72, f32[512,2,128]{2,0,1:T(8,128)S(1)} %convolution_bitcast_fusion), kind=kOutput, calls=%fused_computation.47 | convolution fusion | flops 1572864 | bytes 790528 | tf_op jit(solution)/shard_map/th,thn->tn/dot_general | solution.py:81
  108.4 2.4 fusion.11
  110.8 2.2 multiply_reduce_fusion
  113.1 1.3 rev.13
  114.5 0.9 while.14
  116.6 0.6 reduce-window.16
  118.2 1.3 fusion.29
  119.5 75.2 %psum.7 = f32[2]{0:T(128)S(1)} all-reduce(f32[2]{0:T(128)S(1)} %multiply_reduce_fusion.3), channel_id=1, replica_groups=mesh['dp'=32,'ctx'=8] {'dp','ctx'}, use_global_device_ids=true, to_apply=%region_14.15 | all-reduce | flops 2 | bytes 16 | tf_op jit(solution)/shard_map/psum | solution.py:136
  194.9 21.4 %reduce-scatter.3.cloned.1.call-done = f32[256,256]{1,0:T(8,128)} async-done(((f32[256,8192]{1,0:T(8,128)}), f32[256,256]{1,0:T(8,128)}) %reduce-scatter.3.cloned.1.call-update) | async-done | bytes 262160 | tf_op jit(solution)/shard_map/reduce_scatter | solution.py:130
  216.7 0.8 copy.62
  217.6 1.7 fusion.30
  219.3 0.5 broadcast_multiply_fusion
  219.8 36.1 %reduce-scatter.5.cloned.1.call-done = f32[32,256]{1,0:T(8,128)} async-done(((f32[256,256]{1,0:T(8,128)}), f32[32,256]{1,0:T(8,128)}) %reduce-scatter.5.cloned.1.call-update) | async-done | bytes 32784 | tf_op jit(solution)/shard_map/reduce_scatter | solution.py:131
  (76 shorter events, 6.6 us)
Async XLA Ops:
  7.2 60.4 %all-gather.5.cloned.1.call-start = ((), (), s32[]{:S(2)}) async-start(), calls=%async_computation.2 | async-start | bytes 4718592 | tf_op jit(solution)/shard_map/all_gather | solution.py:118
  7.9 105.2 %all-gather.7.cloned.1.call-start = ((), (), s32[]{:S(2)}) async-start(), calls=%async_computation.5 | async-start | bytes 1179648 | tf_op jit(solution)/shard_map/all_gather | solution.py:11
  11.5 64.2 %copy-start.4 = (bf16[1,512,256]{2,1,0:T(8,128)(2,1)S(1)}, bf16[1,512,256]{2,1,0:T(8,128)(2,1)}, u32[]{:S(2)}) copy-start(bf16[1,512,256]{2,1,0:T(8,128)(2,1)} %param.12) | copy-start | bytes 786436
  11.5 64.5 %copy-start = (bf16[1,512,128]{2,1,0:T(8,128)(2,1)S(1)}, bf16[1,512,128]{2,1,0:T(8,128)(2,1)}, u32[]{:S(2)}) copy-start(bf16[1,512,128]{2,1,0:T(8,128)(2,1)} %param.13) | copy-start | bytes 393220
  11.5 64.5 %copy-start.1 = (bf16[1,512,128]{2,1,0:T(8,128)(2,1)S(1)}, bf16[1,512,128]{2,1,0:T(8,128)(2,1)}, u32[]{:S(2)}) copy-start(bf16[1,512,128]{2,1,0:T(8,128)(2,1)} %param.14) | copy-start | bytes 393220
  74.5 1.8 copy-start.2
  75.7 140.6 %reduce-scatter.3.cloned.1.call-start = ((), (), s32[]{:S(2)}) async-start(), calls=%async_computation.3 | async-start | bytes 8650752 | tf_op jit(solution)/shard_map/reduce_scatter | solution.py:130
  76.0 32.4 %copy-start.5 = (pred[512,512]{1,0:T(8,128)(4,1)}, pred[512,512]{1,0:T(8,128)(4,1)S(1)}, u32[]{:S(2)}) copy-start(pred[512,512]{1,0:T(8,128)(4,1)S(1)} %iota_compare_fusion) | copy-start | bytes 786436
  87.8 168.0 %reduce-scatter.5.cloned.1.call-start = ((), (), s32[]{:S(2)}) async-start(), calls=%async_computation.4 | async-start | bytes 294912 | tf_op jit(solution)/shard_map/reduce_scatter | solution.py:131
  114.4 3.5 %copy-start.7 = (s32[1,512,2]{1,2,0:T(2,128)S(1)}, s32[1,512,2]{1,2,0:T(2,128)}, u32[]{:S(2)}) copy-start(s32[1,512,2]{1,2,0:T(2,128)} %param.15) | copy-start | bytes 12292
  114.5 3.7 %copy-start.6 = (f32[512,1,128]{2,1,0:T(1,128)S(1)}, f32[512,1,128]{2,1,0:T(1,128)}, u32[]{:S(2)}) copy-start(f32[512,1,128]{2,1,0:T(1,128)} %fusion.45) | copy-start | bytes 786436
  115.5 100.8 %copy-start.3 = (f32[512,2,128]{0,2,1:T(8,128)S(1)}, f32[512,2,128]{0,2,1:T(8,128)}, u32[]{:S(2)}) copy-start(f32[512,2,128]{0,2,1:T(8,128)} %fusion.11) | copy-start | bytes 1572868
Sparse Core Ops, SparseCore 0:
  9.8 57.7 all-gather.4
  75.8 37.3 all-gather.6
  117.2 99.0 reduce-scatter.2
  219.4 36.4 reduce-scatter.4
where the time goes:
time: 263 us; the launch traced here: 262 us
  waiting for transfers between devices  114 us (43%)
  blocking collectives  89.9 us (34%)
  matrix products  33.1 us (13%)
  between operations  14 us (5%)
  other arithmetic  5.93 us (2%)
  local copies, waits for them, and re-layouts  4.61 us (2%)
    psum x1, blocking collectives, local(): rate_sum = lax.psum(rate_terms, ('dp', 'ctx'))  75.2 us
    all_gather x1, waiting for transfers between devices, local(): lax.all_gather(out_weight, 'ctx', axis=1, tiled=True)  56.1 us
    reduce_scatter x1, waiting for transfers between devices, local(): lax.psum_scatter(data_part, 'ctx', scatter_dimension=0, tiled=True)  36.1 us
    reduce_scatter x1, waiting for transfers between devices, local(): lax.psum_scatter(local_weight, 'dp', scatter_dimension=1, tiled=True)  21.4 us
    all_gather x1, blocking collectives, carried_in(): pieces = jax.tree.map(lambda part: lax.all_gather(part, axis), value)  14.7 us
    dot_general x1, matrix products, local(): lax.dot_general(outputs, grad_out, (((0,), (0,)), ((), ())), preferred_el...  9.06 us
    dot_general x1, matrix products, local(): lax.dot_general(grad_out, lax.all_gather(out_weight, 'ctx', axis=1, tiled...  6.93 us
  transfers between devices with their start and end apart: 4, of which 4 were waited for; matrix products, arithmetic and copies ran while one was open for 14% of the time, Pallas kernels for 0%

commit v1 on v0

--- a/solution.py
+++ b/solution.py
@@ -1,9 +1,20 @@
+import functools
 import jax
 import jax.numpy as jnp
 from jax import lax
 from jax.sharding import PartitionSpec as P
 
 precise = lax.Precision.HIGHEST
+
+
+def measure_map(values, link_axis):
+    next_value = jnp.stack(lax.axis_size(link_axis) * [values])
+    aux = lax.all_to_all(next_value, link_axis, 0, 0)
+    far_arr = jnp.concatenate(aux, axis=1)
+    return far_arr
+
+
+inputs_search = functools.partial(measure_map, link_axis="ctx")
 
 
 def carried_in(value, axis, join, neutral):
@@ -115,7 +126,7 @@
     length = grad_out.shape[0]
     output_grad = lax.dot_general(
         grad_out,
-        lax.all_gather(out_weight, "ctx", axis=1, tiled=True),
+        inputs_search(out_weight),
         (((1,), (1,)), ((), ())),
         preferred_element_type=jnp.float32,
     ).astype(jnp.bfloat16)

time: 263 us -> 283 us (1.076)
  waiting for transfers between devices: 114 us -> 124 us
  starting transfers between devices: 0.16 us -> 8.72 us
  local copies, waits for them, and re-layouts: 4.61 us -> 8.15 us
    all_to_all x0 -> x1, waiting for transfers between devices: none -> 95 us  [measure_map(): aux = lax.all_to_all(next_value, link_axis, 0, 0)]
    all_gather x1 -> x0, waiting for transfers between devices: 56.1 us -> none  [local(): lax.all_gather(out_weight, 'ctx', axis=1, tiled=True)]
    reduce_scatter x1, waiting for transfers between devices: 21.4 us -> 0.03 us  [local(): lax.psum_scatter(local_weight, 'dp', scatter_dimension=1, tiled=True)]
    all_to_all x0 -> x1, starting transfers between devices: none -> 8.6 us  [measure_map(): aux = lax.all_to_all(next_value, link_axis, 0, 0)]
    reduce_scatter x1, waiting for transfers between devices: 36.1 us -> 29.2 us  [local(): lax.psum_scatter(data_part, 'ctx', scatter_dimension=0, tiled=True)]
  transfers between devices with their start and end apart: 4 -> 4, of which waited for: 4 -> 2; matrix products, arithmetic and copies ran while one was open for 14% -> 12% of each run, Pallas kernels for 0% -> 0%
where the time goes in v1:
time: 283 us
  waiting for transfers between devices  124 us (44%)
  blocking collectives  88.1 us (31%)
  matrix products  34 us (12%)
  between operations  15.7 us (6%)
  starting transfers between devices  8.72 us (3%)
  local copies, waits for them, and re-layouts  8.15 us (3%)
  other arithmetic  3.66 us (1%)
    all_to_all x1, waiting for transfers between devices, measure_map(): aux = lax.all_to_all(next_value, link_axis, 0, 0)  95 us
    psum x1, blocking collectives, local(): rate_sum = lax.psum(rate_terms, ('dp', 'ctx'))  74.3 us
    reduce_scatter x1, waiting for transfers between devices, local(): lax.psum_scatter(data_part, 'ctx', scatter_dimension=0, tiled=True)  29.2 us
    all_gather x1, blocking collectives, carried_in(): pieces = jax.tree.map(lambda part: lax.all_gather(part, axis), value)  13.8 us
    dot_general x1, matrix products, local(): lax.dot_general(outputs, grad_out, (((0,), (0,)), ((), ())), preferred_el...  8.95 us
    all_to_all x1, starting transfers between devices, measure_map(): aux = lax.all_to_all(next_value, link_axis, 0, 0)  8.6 us
    dot_general x1, matrix products, local(): lax.dot_general(grad_out, inputs_search(out_weight), (((1,), (1,)), ((),...  6.99 us
  transfers between devices with their start and end apart: 4, of which 2 were waited for; matrix products, arithmetic and copies ran while one was open for 12% of the time, Pallas kernels for 0%

profile of v1, /device:TPU:2, one launch (start us, length us, event | category | flops | bytes accessed | tf_op | source)
XLA Modules:
  0.0 282.9 jit_solution(13713077421960301664)
XLA Ops:
  8.0 1.2 copy.54
  9.2 2.2 stack.2
  11.5 8.6 %all-to-all-start = ((bf16[8,256,1024]{1,2,0:T(8,128)(2,1)}), bf16[8,256,1024]{1,2,0:T(8,128)(2,1)}, u32[]{:S(2)}, u32[]{:S(2)}) async-start(bf16[8,256,1024]{1,2,0:T(8,128)(2,1)} %stack.2), calls=%async_computation | async-start | bytes 8388608 | tf_op jit(solution)/shard_map/all_to_all | solution.py:12
  20.3 0.6 reduce-window.14
  21.4 95.0 %all-to-all-done = bf16[8,256,1024]{1,2,0:T(8,128)(2,1)} async-done(((bf16[8,256,1024]{1,2,0:T(8,128)(2,1)}), bf16[8,256,1024]{1,2,0:T(8,128)(2,1)}, u32[]{:S(2)}, u32[]{:S(2)}) %all-to-all-start) | async-done | bytes 4194336 | tf_op jit(solution)/shard_map/all_to_all | solution.py:12
  116.5 7.0 %fusion.26 = bf16[512,256]{0,1:T(8,128)(2,1)S(1)} fusion(bf16[256,8192]{0,1:T(8,128)(2,1)} %bitcast.5, bf16[1,512,8192]{2,1,0:T(8,128)(2,1)} %param.10), kind=kOutput, calls=%fused_computation.24 | convolution fusion | flops 2147614720 | bytes 12845056 | tf_op jit(solution)/shard_map/dot_general | solution.py:127
  123.5 1.1 fusion.43
  125.2 0.4 multiply_reduce_fusion.2
  125.7 2.0 fusion.22
  127.7 9.0 %fusion.1 = f32[256,8192]{1,0:T(8,128)} fusion(bf16[512,256]{0,1:T(8,128)(2,1)S(1)} %bitcast.167, bf16[1,512,8192]{2,1,0:T(8,128)(2,1)} %param.10), kind=kOutput, calls=%fused_computation.3 | convolution fusion | flops 2147483648 | bytes 17039360 | tf_op jit(solution)/shard_map/dot_general | solution.py:138
  136.9 13.8 %all-gather.1 = f32[8,1,2]{2,1,0:T(1,128)S(1)} all-gather(f32[1,1,2]{2,1,0:T(1,128)S(1)} %bitcast.178), channel_id=1, replica_groups=mesh['dp'=32,'ctx'=8] {'ctx'}, dimensions={0}, use_global_device_ids=true | all-gather | bytes 72 | tf_op jit(solution)/shard_map/all_gather | solution.py:22
  151.9 4.4 %fusion.45 = f32[512,1,128]{2,1,0:T(1,128)} fusion(f32[512,2,1]{1,2,0:T(1,128)S(1)} %copy.75, f32[512,2,128]{2,0,1:T(8,128)S(1)} %convolution_bitcast_fusion), kind=kOutput, calls=%fused_computation.47 | convolution fusion | flops 1572864 | bytes 790528 | tf_op jit(solution)/shard_map/th,thn->tn/dot_general | solution.py:92
  156.3 2.4 fusion.11
  158.7 2.2 multiply_reduce_fusion
  160.9 1.4 rev.13
  162.3 0.9 while.14
  163.3 0.4 fusion.41
  164.4 0.6 reduce-window.16
  166.0 2.3 fusion.29
  168.2 74.3 %psum.7 = f32[2]{0:T(128)S(1)} all-reduce(f32[2]{0:T(128)S(1)} %multiply_reduce_fusion.3), channel_id=1, replica_groups=mesh['dp'=32,'ctx'=8] {'dp','ctx'}, use_global_device_ids=true, to_apply=%region_14.15 | all-reduce | flops 2 | bytes 16 | tf_op jit(solution)/shard_map/psum | solution.py:147
  243.2 0.8 copy.65
  244.0 1.7 fusion.30
  245.7 0.5 broadcast_multiply_fusion
  246.2 29.2 %reduce-scatter.5.cloned.1.call-done = f32[32,256]{1,0:T(8,128)} async-done(((f32[256,256]{1,0:T(8,128)}), f32[32,256]{1,0:T(8,128)}) %reduce-scatter.5.cloned.1.call-update) | async-done | bytes 32784 | tf_op jit(solution)/shard_map/reduce_scatter | solution.py:142
  (77 shorter events, 5.7 us)
Async XLA Ops:
  11.5 8.6 %copy-start.7 = (f32[2]{0:T(128)S(1)}, f32[2]{0:T(128)}, u32[]{:S(2)}) copy-start(f32[2]{0:T(128)} %param.16) | copy-start | bytes 28
  11.5 8.7 %copy-start.6 = (s32[1,512,2]{1,2,0:T(2,128)S(1)}, s32[1,512,2]{1,2,0:T(2,128)}, u32[]{:S(2)}) copy-start(s32[1,512,2]{1,2,0:T(2,128)} %param.15) | copy-start | bytes 12292
  11.5 9.7 %copy-start.1 = (bf16[1,512,128]{2,1,0:T(8,128)(2,1)S(1)}, bf16[1,512,128]{2,1,0:T(8,128)(2,1)}, u32[]{:S(2)}) copy-start(bf16[1,512,128]{2,1,0:T(8,128)(2,1)} %param.14) | copy-start | bytes 393220
  11.5 105.0 %all-to-all-start = ((bf16[8,256,1024]{1,2,0:T(8,128)(2,1)}), bf16[8,256,1024]{1,2,0:T(8,128)(2,1)}, u32[]{:S(2)}, u32[]{:S(2)}) async-start(bf16[8,256,1024]{1,2,0:T(8,128)(2,1)} %stack.2), calls=%async_computation | async-start | bytes 8388608 | tf_op jit(solution)/shard_map/all_to_all | solution.py:12
  20.1 140.8 %all-gather.4.cloned.1.call-start = ((), (), s32[]{:S(2)}) async-start(), calls=%async_computation.5 | async-start | bytes 1179648 | tf_op jit(solution)/shard_map/all_gather | solution.py:22
  116.5 8.2 %copy-start.4 = (bf16[1,512,256]{2,1,0:T(8,128)(2,1)S(1)}, bf16[1,512,256]{2,1,0:T(8,128)(2,1)}, u32[]{:S(2)}) copy-start(bf16[1,512,256]{2,1,0:T(8,128)(2,1)} %param.12) | copy-start | bytes 786436
  116.5 8.4 %copy-start = (bf16[1,512,128]{2,1,0:T(8,128)(2,1)S(1)}, bf16[1,512,128]{2,1,0:T(8,128)(2,1)}, u32[]{:S(2)}) copy-start(bf16[1,512,128]{2,1,0:T(8,128)(2,1)} %param.13) | copy-start | bytes 393220
  123.5 1.7 copy-start.2
  124.6 118.1 %reduce-scatter.3.cloned.1.call-start = ((), (), s32[]{:S(2)}) async-start(), calls=%async_computation.3 | async-start | bytes 8650752 | tf_op jit(solution)/shard_map/reduce_scatter | solution.py:141
  124.9 31.4 %copy-start.5 = (pred[512,512]{1,0:T(8,128)(4,1)}, pred[512,512]{1,0:T(8,128)(4,1)S(1)}, u32[]{:S(2)}) copy-start(pred[512,512]{1,0:T(8,128)(4,1)S(1)} %iota_compare_fusion) | copy-start | bytes 786436
  136.6 138.8 %reduce-scatter.5.cloned.1.call-start = ((), (), s32[]{:S(2)}) async-start(), calls=%async_computation.4 | async-start | bytes 294912 | tf_op jit(solution)/shard_map/reduce_scatter | solution.py:142
  163.3 79.5 %copy-start.3 = (f32[512,2,128]{0,2,1:T(8,128)S(1)}, f32[512,2,128]{0,2,1:T(8,128)}, u32[]{:S(2)}) copy-start(f32[512,2,128]{0,2,1:T(8,128)} %fusion.11) | copy-start | bytes 1572868
Sparse Core Ops, SparseCore 0:
  124.7 35.0 all-gather.3
  242.9 32.5 reduce-scatter.4
Sparse Core Ops, SparseCore 1:
  136.7 96.3 reduce-scatter.2
